TPU v7x, 32 devices: a whole 2x2x4 slice. The times are simulated.
32 devices in a mesh: groups: 2 (over y), wide: 4 (over z), narrow: 4 (over x, core).
Axes of the slice: x: 2, y: 2, z: 4, core: 2. Of those that a mesh axis runs over, the one named last changes fastest.
Arguments:
- residual: bfloat16 [512, 4096], P(('groups', 'wide')), parts along dimension 0, may hold values from -6 to 6
- query_rows: bfloat16 [512, 4096], P(('groups', 'wide'), 'narrow'), parts along dimension 0, may hold values from -160 to 160
- key_rows: bfloat16 [512, 4096], P(('groups', 'wide'), 'narrow'), parts along dimension 0, may hold values from -160 to 160
- value_rows: bfloat16 [512, 4096], P(('groups', 'wide'), 'narrow'), parts along dimension 0, may hold values from -6 to 6
- segment_ids: int32 [8, 64], P(('groups', 'wide')), parts along dimension 0, may hold values from 0 to 3, never falling along the last dimension, each value on 1 to 32 neighbouring positions
- o_weight: bfloat16 [4096, 4096], P('narrow', 'wide'), may hold values from -0.09375 to 0.09375
- norm_gain: float32 [4096], replicated, may hold values from 0.1 to 1.9
- w_gate: bfloat16 [32, 4096, 1024], P('wide', None, 'narrow'), may hold values from -0.09375 to 0.09375
- w_up: bfloat16 [32, 4096, 1024], P('wide', None, 'narrow'), may hold values from -0.09375 to 0.09375
- w_down: bfloat16 [32, 1024, 4096], P('wide', None, 'narrow'), may hold values from -0.1875 to 0.1875
- expert_ids: int32 [512, 8], P(('groups', 'wide')), parts along dimension 0, may hold values from 0 to 31, all different within a row; in each aligned block of 16 rows (0 to 15, 16 to 31, ...) at most 8 rows name the same one
- gate_weights: float32 [512, 8], P(('groups', 'wide')), parts along dimension 0, may hold values from 0.05 to 1
- target: bfloat16 [512, 4096], P(('groups', 'wide', 'narrow')), parts along dimension 0, may hold values from -6 to 6
Outputs:
- errors: float32 [512], P(('groups', 'wide', 'narrow')), parts along dimension 0
There are 2 independent parts, one for each index of `groups`. A program takes and returns all parts, laid end to end along the dimension named above; an argument that names none is the same for every part. Nothing has to cross between parts.
Inputs may be any that keep to these rules, and one draw needn't show every extreme that they name: `expert_ids`: in each aligned block of 16 rows (the rows of one device) no expert is named more than 8 times, a bound that some block reaches. `segment_ids`: along each row the trajectory number never falls; a trajectory covers 1 to 32 positions.
All inputs are finite; a program needn't handle non-finite values.
Results may differ from a plain program's by a relative error of at most 0.0005.
Values may be sent and summed in bfloat16 or wider, within the bound.
No kernel may reach another device: no remote copies, remote signals or barrier semaphores. Data moves between devices by JAX's collectives and lax.ppermute only.
A program may use at most 128 MiB of HBM per device.

v0:
```python
import jax
import jax.numpy as jnp
from jax import lax
from jax.sharding import PartitionSpec as P

HD = 128
EXPERTS = 32
TOP = 8


def attend(query_block, key_block, value_block, seg_row):
    tok_count = query_block.shape[0]
    head_count = query_block.shape[1] // HD
    query_heads = query_block.reshape(tok_count, head_count, HD)
    key_heads = key_block.reshape(tok_count, head_count, HD)
    value_heads = value_block.reshape(tok_count, head_count, HD)
    scores = jnp.einsum(
        "qhd,khd->hqk", query_heads, key_heads, preferred_element_type=jnp.float32
    ) * HD ** (-0.5)
    places = jnp.arange(tok_count, dtype=jnp.int32)
    allowed = (seg_row[:, None] == seg_row[None, :]) & (places[None, :] <= places[:, None])
    scores = jnp.where(allowed[None], scores, -jnp.inf)
    peak_score = jnp.max(scores, axis=2, keepdims=True)
    weights = jnp.exp(scores - peak_score)
    denom_sum = jnp.sum(weights, axis=2, keepdims=True)
    mixed_out = jnp.einsum(
        "hqk,khd->qhd",
        weights.astype(jnp.bfloat16),
        value_heads,
        preferred_element_type=jnp.float32,
    )
    mixed_out = mixed_out / jnp.transpose(denom_sum, (1, 0, 2))
    return mixed_out.reshape(tok_count, -1).astype(jnp.bfloat16)


def normalize(stream_rows, gain_vector):
    mean_sq = jnp.mean(stream_rows * stream_rows, axis=1, keepdims=True)
    return (stream_rows * lax.rsqrt(mean_sq + 1e-06) * gain_vector).astype(jnp.bfloat16)


def slot_positions(expert_list):
    row_count, route_count = expert_list.shape
    flat_ids = expert_list.reshape(-1)
    onehot = (flat_ids[:, None] == jnp.arange(EXPERTS, dtype=jnp.int32)[None, :]).astype(jnp.int32)
    before = jnp.cumsum(onehot, axis=0) - onehot
    return jnp.sum(before * onehot, axis=1).reshape(row_count, route_count)


def fill_slots(row_data, slot_index, row_index, slot_total):
    source = (
        jnp.full((slot_total,), -1, jnp.int32).at[slot_index.reshape(-1)].set(row_index.reshape(-1))
    )
    picked = row_data[jnp.maximum(source, 0)]
    return jnp.where((source >= 0)[:, None], picked, jnp.zeros((), row_data.dtype))


def body(
    residual,
    query_rows,
    key_rows,
    value_rows,
    segment_ids,
    o_weight,
    norm_gain,
    w_gate,
    w_up,
    w_down,
    expert_ids,
    gate_weights,
    target,
):
    wide_count = lax.axis_size("wide")
    narrow_count = lax.axis_size("narrow")
    narrow_here = lax.axis_index("narrow")
    tok_count = query_rows.shape[0]
    row_count = tok_count // narrow_count
    capacity = max(2, 2 * row_count * TOP // EXPERTS)
    local_experts = w_gate.shape[0]
    model_width = residual.shape[1]
    attended = attend(query_rows, key_rows, value_rows, segment_ids[0])
    partial_mix = jnp.dot(
        attended,
        lax.all_gather(o_weight, "wide", axis=1, tiled=True),
        preferred_element_type=jnp.float32,
    )
    own_ids = lax.dynamic_slice_in_dim(expert_ids, narrow_here * row_count, row_count, 0)
    own_gates = lax.dynamic_slice_in_dim(gate_weights, narrow_here * row_count, row_count, 0)
    mixed_own = lax.psum_scatter(partial_mix, "narrow", scatter_dimension=0, tiled=True)
    own_resid = lax.dynamic_slice_in_dim(residual, narrow_here * row_count, row_count, 0)
    stream = own_resid.astype(jnp.float32) + mixed_own
    normed_own = normalize(stream, norm_gain)
    own_pos = slot_positions(own_ids)
    slot_index = own_ids * capacity + own_pos
    row_index = jnp.broadcast_to(jnp.arange(row_count, dtype=jnp.int32)[:, None], own_ids.shape)
    outgoing = fill_slots(normed_own, slot_index, row_index, EXPERTS * capacity)
    incoming = lax.all_to_all(
        outgoing.reshape(wide_count, -1, model_width),
        "wide",
        split_axis=0,
        concat_axis=0,
        tiled=True,
    )
    incoming = incoming.reshape(wide_count, local_experts, 1, capacity, model_width)
    grouped = lax.all_gather(incoming, "narrow", axis=2, tiled=True)
    expert_rows = grouped.reshape(wide_count, local_experts, narrow_count * capacity, model_width)
    gate_val = jnp.einsum("wesd,edh->wesh", expert_rows, w_gate, preferred_element_type=jnp.float32)
    up_val = jnp.einsum("wesd,edh->wesh", expert_rows, w_up, preferred_element_type=jnp.float32)
    hidden = (jax.nn.silu(gate_val) * up_val).astype(jnp.bfloat16)
    slice_width = w_down.shape[2]
    outcome = jnp.einsum(
        "wesh,ehd->wesd",
        lax.all_gather(hidden, "narrow", axis=3, tiled=True),
        w_down,
        preferred_element_type=jnp.float32,
    ).astype(jnp.bfloat16)
    outcome = outcome.reshape(wide_count, local_experts, narrow_count, capacity, slice_width)
    returned = lax.all_to_all(
        lax.all_to_all(outcome, "wide", split_axis=0, concat_axis=0, tiled=True),
        "narrow",
        split_axis=2,
        concat_axis=4,
        tiled=True,
    )
    returned = returned.reshape(EXPERTS * capacity, model_width)
    chosen = returned[own_ids * capacity + own_pos]
    moe_sum = jnp.sum(own_gates[:, :, None] * chosen.astype(jnp.float32), axis=1)
    predicted = stream + moe_sum
    return jnp.mean((predicted - target.astype(jnp.float32)) ** 2, axis=1)


def solution(mesh):
    return jax.shard_map(
        body,
        mesh=mesh,
        in_specs=(
            P(("groups", "wide"), None),
            P(("groups", "wide"), "narrow"),
            P(("groups", "wide"), "narrow"),
            P(("groups", "wide"), "narrow"),
            P(("groups", "wide"), None),
            P("narrow", "wide"),
            P(),
            P("wide", None, "narrow"),
            P("wide", None, "narrow"),
            P("wide", None, "narrow"),
            P(("groups", "wide"), None),
            P(("groups", "wide"), None),
            P(("groups", "wide", "narrow"), None),
        ),
        out_specs=P(("groups", "wide", "narrow")),
        check_vma=False,
    )
```

profile of v0, /device:TPU:0, one launch (start us, length us, event | category | flops | bytes accessed | tf_op | source)
XLA Modules:
  0.0 455.0 jit_solution(6789663493847794399)
XLA Ops:
  7.3 0.8 fusion.51
  8.1 1.2 fusion.55
  9.7 151.6 %all-gather.4.cloned.1.call-done = bf16[1024,4096]{1,0:T(8,128)(2,1)} async-done(((bf16[1024,1024]{1,0:T(8,128)(2,1)}), bf16[1024,4096]{1,0:T(8,128)(2,1)}) %all-gather.4.cloned.1.call-update) | async-done | bytes 8388624 | tf_op jit(solution)/shard_map/all_gather | solution.py:83
  161.3 6.0 %fusion.40 = f32[64,4096]{1,0:T(8,128)} fusion(bf16[1024,4096]{1,0:T(8,128)(2,1)} %all-gather.4.cloned.1.call-done, bf16[8,8,8,128]{3,2,1,0:T(8,128)(2,1)S(1)} %fusion.36), kind=kOutput, calls=%fused_computation.34 | convolution fusion | flops 536870912 | bytes 9568256 | tf_op jit(solution)/shard_map/dot_general | solution.py:81
  168.4 1.0 scatter_custom_fusion
  169.5 21.0 %reduce-scatter.2.cloned.1.call-done = f32[16,4096]{1,0:T(8,128)} async-done(((f32[64,4096]{1,0:T(8,128)}), f32[16,4096]{1,0:T(8,128)}) %reduce-scatter.2.cloned.1.call-update) | async-done | bytes 262160 | tf_op jit(solution)/shard_map/reduce_scatter | solution.py:88
  190.5 1.1 multiply_reduce_fusion.1
  191.6 1.0 multiply_convert_fusion
  192.6 1.8 gather_fusion
  194.7 52.5 %all_to_all.25 = bf16[4,64,4096]{2,1,0:T(8,128)(2,1)} all-to-all(bf16[4,64,4096]{2,1,0:T(8,128)(2,1)S(1)} %broadcast_select_fusion), channel_id=1, replica_groups=mesh['groups'=2,'wide'=4,'narrow'=4] {'wide'}, dimensions={0} | all-to-all | bytes 4194304 | tf_op jit(solution)/shard_map/all_to_all | solution.py:96
  247.5 56.3 %all-gather.6.cloned.1.call-done = bf16[4,8,4,8,4096]{4,3,1,0,2:T(8,128)(2,1)} async-done(((bf16[4,8,1,8,4096]{4,3,1,0,2:T(8,128)(2,1)}), bf16[4,8,4,8,4096]{4,3,1,0,2:T(8,128)(2,1)}) %all-gather.6.cloned.1.call-update) | async-done | bytes 8388624 | tf_op jit(solution)/shard_map/all_gather | solution.py:104
  303.8 10.5 %fusion.13 = f32[4,8,32,256]{3,2,0,1:T(8,128)S(1)} fusion(bf16[8,4096,256]{2,1,0:T(8,128)(2,1)} %param.20, bf16[4,8,4,8,4096]{4,3,1,0,2:T(8,128)(2,1)} %all-gather.6.cloned.1.call-done), kind=kOutput, calls=%fused_computation.17 | convolution fusion | flops 2147483648 | bytes 26214400 | tf_op jit(solution)/shard_map/wesd,edh->wesh/dot_general | solution.py:106
  314.3 11.5 %fusion.28 = bf16[4,8,32,256]{3,2,0,1:T(8,128)(2,1)} fusion(bf16[8,4096,256]{2,1,0:T(8,128)(2,1)} %param.21, bf16[4,8,4,8,4096]{4,3,1,0,2:T(8,128)(2,1)} %all-gather.6.cloned.1.call-done, f32[4,8,32,256]{3,2,0,1:T(8,128)S(1)} %fusion.13), kind=kOutput, calls=%fused_computation.20 | convolution fusion | flops 2149056512 | bytes 26738688 | tf_op jit(solution)/shard_map/wesd,edh->wesh/dot_general | solution.py:107
  325.8 23.0 %all-gather.8.cloned.1.call-done = bf16[4,8,32,1024]{3,2,0,1:T(8,128)(2,1)} async-done(((bf16[4,8,32,256]{3,2,0,1:T(8,128)(2,1)}), bf16[4,8,32,1024]{3,2,0,1:T(8,128)(2,1)}) %all-gather.8.cloned.1.call-update) | async-done | bytes 2097168 | tf_op jit(solution)/shard_map/all_gather | solution.py:112
  348.8 8.8 %convert_bitcast_fusion = bf16[4,8,4,8,1024]{4,3,2,0,1:T(8,128)(2,1)S(1)} fusion(bf16[4,8,32,1024]{3,2,0,1:T(8,128)(2,1)} %all-gather.8.cloned.1.call-done, bf16[8,1024,1024]{2,1,0:T(8,128)(2,1)} %param.22), kind=kOutput, calls=%fused_computation.15 | convolution fusion | flops 2148532224 | bytes 20971520 | tf_op jit(solution)/shard_map/wesh,ehd->wesd/dot_general | solution.py:110
  357.8 53.0 %all_to_all.26 = bf16[4,8,4,8,1024]{4,3,2,1,0:T(8,128)(2,1)S(1)} all-to-all(bf16[4,8,4,8,1024]{4,3,2,1,0:T(8,128)(2,1)S(1)} %copy.38), channel_id=1, replica_groups=mesh['groups'=2,'wide'=4,'narrow'=4] {'wide'}, dimensions={0} | all-to-all | bytes 4194304 | tf_op jit(solution)/shard_map/all_to_all | solution.py:118
  410.8 1.5 copy.39
  412.3 3.6 all-to-all-start.2
  416.2 25.4 %all-to-all-done.2 = bf16[4,8,4,8,1024]{4,3,0,1,2:T(8,128)(2,1)S(1)} async-done(((bf16[4,8,4,8,1024]{4,3,0,1,2:T(8,128)(2,1)}), bf16[4,8,4,8,1024]{4,3,0,1,2:T(8,128)(2,1)S(1)}, u32[]{:S(2)}, u32[]{:S(2)}) %all-to-all-start.2) | async-done | bytes 2097184 | tf_op jit(solution)/shard_map/all_to_all | solution.py:117
  441.5 1.3 copy-done.2
  442.9 1.8 copy.40
  444.7 1.2 gather_fusion.1
  445.9 0.8 fusion.10
  446.7 1.2 multiply_reduce_fusion
  (49 shorter events, 3.6 us)
Async XLA Ops:
  6.5 2.8 copy-start
  6.5 154.7 %all-gather.4.cloned.1.call-start = ((), (), s32[]{:S(2)}) async-start(), calls=%async_computation.4 | async-start | bytes 10485760 | tf_op jit(solution)/shard_map/all_gather | solution.py:83
  7.3 183.2 %reduce-scatter.2.cloned.1.call-start = ((), (), s32[]{:S(2)}) async-start(), calls=%async_computation.5 | async-start | bytes 1310720 | tf_op jit(solution)/shard_map/reduce_scatter | solution.py:88
  9.6 157.7 %copy-start.6 = (s32[64,8]{0,1:T(8,128)S(1)}, s32[64,8]{0,1:T(8,128)}, u32[]{:S(2)}) copy-start(s32[64,8]{0,1:T(8,128)} %param.23) | copy-start | bytes 6148
  9.6 180.8 %copy-start.4 = (bf16[64,4096]{1,0:T(8,128)(2,1)S(1)}, bf16[64,4096]{1,0:T(8,128)(2,1)}, u32[]{:S(2)}) copy-start(bf16[64,4096]{1,0:T(8,128)(2,1)} %param.13) | copy-start | bytes 1572868
  9.7 181.9 %copy-start.5 = (f32[4096]{0:T(1024)S(1)}, f32[4096]{0:T(1024)}, u32[]{:S(2)}) copy-start(f32[4096]{0:T(1024)} %param.19) | copy-start | bytes 49156
  167.3 136.5 %all-gather.6.cloned.1.call-start = ((), (), s32[]{:S(2)}) async-start(), calls=%async_computation.6 | async-start | bytes 10485760 | tf_op jit(solution)/shard_map/all_gather | solution.py:104
  247.3 101.5 %all-gather.8.cloned.1.call-start = ((), (), s32[]{:S(2)}) async-start(), calls=%async_computation.7 | async-start | bytes 2621440 | tf_op jit(solution)/shard_map/all_gather | solution.py:112
  410.8 5.2 %copy-start.7 = (f32[64,8]{0,1:T(8,128)S(1)}, f32[64,8]{0,1:T(8,128)}, u32[]{:S(2)}) copy-start(f32[64,8]{0,1:T(8,128)} %param.24) | copy-start | bytes 6148
  412.3 29.2 %all-to-all-start.2 = ((bf16[4,8,4,8,1024]{4,3,0,1,2:T(8,128)(2,1)}), bf16[4,8,4,8,1024]{4,3,0,1,2:T(8,128)(2,1)S(1)}, u32[]{:S(2)}, u32[]{:S(2)}) async-start(bf16[4,8,4,8,1024]{4,3,0,1,2:T(8,128)(2,1)} %copy.39), calls=%async_computation.3 | async-start | bytes 4194304 | tf_op jit(solution)/shard_map/all_to_all | solution.py:117
  441.5 1.4 copy-start.2
  444.7 3.7 copy-start.1
  444.7 2.0 copy-start.3
Sparse Core Ops, SparseCore 0:
  8.9 152.3 all-gather.3
  167.4 22.9 reduce-scatter.1
  247.4 56.3 all-gather.5
  325.9 22.8 all-gather.7
where the time goes:
time: 455 us
  waiting for transfers between devices  278 us (61%)
  blocking collectives  106 us (23%)
  matrix products  38.2 us (8%)
  between operations  13.4 us (3%)
  local copies, waits for them, and re-layouts  9.75 us (2%)
  other arithmetic  6.17 us (1%)
    all_gather x1, waiting for transfers between devices, body(): lax.all_gather(o_weight, 'wide', axis=1, tiled=True)  152 us
    all_gather x1, waiting for transfers between devices, body(): grouped = lax.all_gather(incoming, 'narrow', axis=2, tiled=True)  56.3 us
    all_to_all x1, blocking collectives, body(): lax.all_to_all(outcome, 'wide', split_axis=0, concat_axis=0, tiled=True)  53 us
    all_to_all x1, blocking collectives, body(): lax.all_to_all(outgoing.reshape(wide_count, -1, model_width), 'wide', spl...  52.5 us
    all_to_all x1, waiting for transfers between devices, body(): lax.all_to_all(lax.all_to_all(outcome, 'wide', split_axis=0, concat_axis=...  25.4 us
    all_gather x1, waiting for transfers between devices, body(): lax.all_gather(hidden, 'narrow', axis=3, tiled=True)  23 us
    reduce_scatter x1, waiting for transfers between devices, body(): lax.psum_scatter(partial_mix, 'narrow', scatter_dimension=0, tiled=True)  21 us
    dot_general x1, matrix products, body(): jnp.einsum('wesd,edh->wesh', expert_rows, w_up, preferred_element_type=jn...  11.5 us
  transfers between devices with their start and end apart: 5, of which 5 were waited for; matrix products, arithmetic and copies ran while one was open for 1% of the time, Pallas kernels for 0%

commit v1 on v0

--- a/solution.py
+++ b/solution.py
@@ -6,6 +6,23 @@
 HD = 128
 EXPERTS = 32
 TOP = 8
+
+
+def in_order(blocks, dim):
+    blocks = jnp.moveaxis(blocks, 0, dim)
+    lengths = blocks.shape
+    return blocks.reshape(*lengths[:dim], lengths[dim] * lengths[dim + 1], *lengths[dim + 2 :])
+
+
+def collect(x, axis, dim):
+    devices = lax.axis_size(axis)
+    right = [(i, (i + 1) % devices) for i in range(devices)]
+    blocks = [x]
+    while len(blocks) < devices:
+        blocks.append(lax.ppermute(blocks[-1], axis, right))
+    index = lax.axis_index(axis)
+    blocks = jnp.stack(blocks)[(index - jnp.arange(devices)) % devices]
+    return in_order(blocks, dim)
 
 
 def attend(query_block, key_block, value_block, seg_row):
@@ -101,7 +118,7 @@
         tiled=True,
     )
     incoming = incoming.reshape(wide_count, local_experts, 1, capacity, model_width)
-    grouped = lax.all_gather(incoming, "narrow", axis=2, tiled=True)
+    grouped = collect(incoming, "narrow", 2)
     expert_rows = grouped.reshape(wide_count, local_experts, narrow_count * capacity, model_width)
     gate_val = jnp.einsum("wesd,edh->wesh", expert_rows, w_gate, preferred_element_type=jnp.float32)
     up_val = jnp.einsum("wesd,edh->wesh", expert_rows, w_up, preferred_element_type=jnp.float32)

time: 455 us -> 492 us (1.081)
  waiting for transfers between devices: 278 us -> 296 us
  local copies, waits for them, and re-layouts: 9.75 us -> 23.5 us
    ppermute x0 -> x3, waiting for transfers between devices: none -> 76.3 us  [collect(): blocks.append(lax.ppermute(blocks[-1], axis, right))]
    all_gather x1 -> x0, waiting for transfers between devices: 56.3 us -> none  [body(): grouped = lax.all_gather(incoming, 'narrow', axis=2, tiled=True)]
    gather x0 -> x3, local copies, waits for them, and re-layouts: none -> 13.7 us  [collect(): blocks = jnp.stack(blocks)[(index - jnp.arange(devices)) % devices]]
  transfers between devices with their start and end apart: 5 -> 7, of which waited for: 5 -> 7; matrix products, arithmetic and copies ran while one was open for 1% -> 1% of each run, Pallas kernels for 0% -> 0%
where the time goes in v1:
time: 492 us
  waiting for transfers between devices  296 us (60%)
  blocking collectives  105 us (21%)
  matrix products  42.4 us (9%)
  local copies, waits for them, and re-layouts  23.5 us (5%)
  between operations  13.4 us (3%)
  other arithmetic  7.29 us (1%)
    all_gather x1, waiting for transfers between devices, body(): lax.all_gather(o_weight, 'wide', axis=1, tiled=True)  152 us
    ppermute x3, waiting for transfers between devices, collect(): blocks.append(lax.ppermute(blocks[-1], axis, right))  76.3 us
    all_to_all x1, blocking collectives, body(): lax.all_to_all(outcome, 'wide', split_axis=0, concat_axis=0, tiled=True)  53 us
    all_to_all x1, blocking collectives, body(): lax.all_to_all(outgoing.reshape(wide_count, -1, model_width), 'wide', spl...  52.4 us
    all_to_all x1, waiting for transfers between devices, body(): lax.all_to_all(lax.all_to_all(outcome, 'wide', split_axis=0, concat_axis=...  25.4 us
    all_gather x1, waiting for transfers between devices, body(): lax.all_gather(hidden, 'narrow', axis=3, tiled=True)  21.1 us
    reduce_scatter x1, waiting for transfers between devices, body(): lax.psum_scatter(partial_mix, 'narrow', scatter_dimension=0, tiled=True)  21 us
    gather x3, local copies, waits for them, and re-layouts, collect(): blocks = jnp.stack(blocks)[(index - jnp.arange(devices)) % devices]  13.7 us
  transfers between devices with their start and end apart: 7, of which 7 were waited for; matrix products, arithmetic and copies ran while one was open for 1% of the time, Pallas kernels for 0%

profile of v1, /device:TPU:0, one launch (start us, length us, event | category | flops | bytes accessed | tf_op | source)
XLA Modules:
  0.0 491.8 jit_solution(10833004847604854866)
XLA Ops:
  8.1 1.2 fusion.57
  9.7 151.6 %all-gather.3.cloned.1.call-done = bf16[1024,4096]{1,0:T(8,128)(2,1)} async-done(((bf16[1024,1024]{1,0:T(8,128)(2,1)}), bf16[1024,4096]{1,0:T(8,128)(2,1)}) %all-gather.3.cloned.1.call-update) | async-done | bytes 8388624 | tf_op jit(solution)/shard_map/all_gather | solution.py:100
  161.3 6.0 %fusion.40 = f32[64,4096]{1,0:T(8,128)} fusion(bf16[1024,4096]{1,0:T(8,128)(2,1)} %all-gather.3.cloned.1.call-done, bf16[8,8,8,128]{3,2,1,0:T(8,128)(2,1)S(1)} %fusion.36), kind=kOutput, calls=%fused_computation.40 | convolution fusion | flops 536870912 | bytes 9568256 | tf_op jit(solution)/shard_map/dot_general | solution.py:98
  169.5 21.0 %reduce-scatter.2.cloned.1.call-done = f32[16,4096]{1,0:T(8,128)} async-done(((f32[64,4096]{1,0:T(8,128)}), f32[16,4096]{1,0:T(8,128)}) %reduce-scatter.2.cloned.1.call-update) | async-done | bytes 262160 | tf_op jit(solution)/shard_map/reduce_scatter | solution.py:105
  192.6 1.8 gather_fusion
  194.7 52.4 %all_to_all.25 = bf16[4,64,4096]{2,1,0:T(8,128)(2,1)S(1)} all-to-all(bf16[4,64,4096]{2,1,0:T(8,128)(2,1)S(1)} %broadcast_select_fusion), channel_id=1, replica_groups=mesh['groups'=2,'wide'=4,'narrow'=4] {'wide'}, dimensions={0} | all-to-all | bytes 4194304 | tf_op jit(solution)/shard_map/all_to_all | solution.py:113
  247.1 25.5 %collective-permute-done = bf16[4,8,1,8,4096]{4,3,1,0,2:T(8,128)(2,1)S(1)} collective-permute-done((bf16[4,8,1,8,4096]{4,3,1,0,2:T(8,128)(2,1)S(1)}, bf16[4,8,1,8,4096]{4,3,1,0,2:T(8,128)(2,1)S(1)}, u32[]{:S(2)}, u32[]{:S(2)}) %collective-permute-start) | collective-permute-done | bytes 2097184 | tf_op jit(solution)/shard_map/ppermute | solution.py:22
  272.6 25.5 %collective-permute-done.1 = bf16[4,8,1,8,4096]{4,3,1,0,2:T(8,128)(2,1)S(1)} collective-permute-done((bf16[4,8,1,8,4096]{4,3,1,0,2:T(8,128)(2,1)S(1)}, bf16[4,8,1,8,4096]{4,3,1,0,2:T(8,128)(2,1)S(1)}, u32[]{:S(2)}, u32[]{:S(2)}) %collective-permute-start.1) | collective-permute-done | bytes 2097184 | tf_op jit(solution)/shard_map/ppermute | solution.py:22
  298.1 25.4 %collective-permute-done.2 = bf16[4,8,1,8,4096]{4,3,1,0,2:T(8,128)(2,1)S(1)} collective-permute-done((bf16[4,8,1,8,4096]{4,3,1,0,2:T(8,128)(2,1)S(1)}, bf16[4,8,1,8,4096]{4,3,1,0,2:T(8,128)(2,1)S(1)}, u32[]{:S(2)}, u32[]{:S(2)}) %collective-permute-start.2) | collective-permute-done | bytes 2097184 | tf_op jit(solution)/shard_map/ppermute | solution.py:22
  324.6 3.8 slice_bitcast_fusion.1
  328.5 4.9 %gather_fusion.2 = bf16[4,4,8,8,2048]{4,3,2,1,0:T(8,128)(2,1)} fusion(bf16[4,4,8,8,2048]{4,3,2,1,0:T(8,128)(2,1)} %get-tuple-element.7, s32[1024]{0:T(1024)S(1)} %pad_clamp_fusion.1), kind=kCustom, calls=%fused_computation.2 | custom fusion | bytes 8388624 | tf_op jit(solution)/shard_map/gather | solution.py:24
  333.4 5.0 %gather_fusion.3 = bf16[4,4,8,8,2048]{4,3,2,1,0:T(8,128)(2,1)} fusion(bf16[4,4,8,8,2048]{4,3,2,1,0:T(8,128)(2,1)} %get-tuple-element.8, s32[1024]{0:T(1024)S(1)} %pad_clamp_fusion.1), kind=kCustom, calls=%fused_computation.3 | custom fusion | bytes 8388624 | tf_op jit(solution)/shard_map/gather | solution.py:24
  338.4 12.6 %fusion.13 = f32[4,8,32,256]{3,2,0,1:T(8,128)S(1)} fusion(bf16[8,4096,256]{2,1,0:T(8,128)(2,1)} %param.20, bf16[4,4,8,1,8,2048]{5,4,2,1,0,3:T(8,128)(2,1)} %bitcast.136, bf16[4,4,8,1,8,2048]{5,4,2,1,0,3:T(8,128)(2,1)} %bitcast.134), kind=kOutput, calls=%fused_computation.23 | convolution fusion | flops 2164260864 | bytes 26214400 | tf_op jit(solution)/shard_map/wesd,edh->wesh/dot_general | solution.py:123
  351.0 13.5 %fusion.28 = bf16[4,8,32,256]{3,2,0,1:T(8,128)(2,1)} fusion(bf16[8,4096,256]{2,1,0:T(8,128)(2,1)} %param.21, f32[4,8,32,256]{3,2,0,1:T(8,128)S(1)} %fusion.13, bf16[4,4,8,1,8,2048]{5,4,2,1,0,3:T(8,128)(2,1)} %bitcast.137, bf16[4,4,8,1,8,2048]{5,4,2,1,0,3:T(8,128)(2,1)} %bitcast.135), kind=kOutput, calls=%fused_computation.26 | convolution fusion | flops 2165833728 | bytes 26738688 | tf_op jit(solution)/shard_map/wesd,edh->wesh/dot_general | solution.py:124
  364.5 21.1 %all-gather.5.cloned.1.call-done = bf16[4,8,32,1024]{3,2,0,1:T(8,128)(2,1)} async-done(((bf16[4,8,32,256]{3,2,0,1:T(8,128)(2,1)}), bf16[4,8,32,1024]{3,2,0,1:T(8,128)(2,1)}) %all-gather.5.cloned.1.call-update) | async-done | bytes 2097168 | tf_op jit(solution)/shard_map/all_gather | solution.py:129
  385.7 8.8 %convert_bitcast_fusion = bf16[4,8,4,8,1024]{4,3,2,0,1:T(8,128)(2,1)S(1)} fusion(bf16[4,8,32,1024]{3,2,0,1:T(8,128)(2,1)} %all-gather.5.cloned.1.call-done, bf16[8,1024,1024]{2,1,0:T(8,128)(2,1)} %param.22), kind=kOutput, calls=%fused_computation.21 | convolution fusion | flops 2148532224 | bytes 20971520 | tf_op jit(solution)/shard_map/wesh,ehd->wesd/dot_general | solution.py:127
  394.6 53.0 %all_to_all.26 = bf16[4,8,4,8,1024]{4,3,2,1,0:T(8,128)(2,1)S(1)} all-to-all(bf16[4,8,4,8,1024]{4,3,2,1,0:T(8,128)(2,1)S(1)} %copy.42), channel_id=1, replica_groups=mesh['groups'=2,'wide'=4,'narrow'=4] {'wide'}, dimensions={0} | all-to-all | bytes 4194304 | tf_op jit(solution)/shard_map/all_to_all | solution.py:135
  447.6 1.5 copy.43
  449.2 3.6 all-to-all-start.2
  453.0 25.4 %all-to-all-done.2 = bf16[4,8,4,8,1024]{4,3,0,1,2:T(8,128)(2,1)S(1)} async-done(((bf16[4,8,4,8,1024]{4,3,0,1,2:T(8,128)(2,1)}), bf16[4,8,4,8,1024]{4,3,0,1,2:T(8,128)(2,1)S(1)}, u32[]{:S(2)}, u32[]{:S(2)}) %all-to-all-start.2) | async-done | bytes 2097184 | tf_op jit(solution)/shard_map/all_to_all | solution.py:134
  478.4 1.3 copy-done.2
  479.8 1.8 copy.44
  481.6 1.2 gather_fusion.1
  483.6 1.2 multiply_reduce_fusion
  (58 shorter events, 9.2 us)
Async XLA Ops:
  6.5 2.8 copy-start
  6.5 154.7 %all-gather.3.cloned.1.call-start = ((), (), s32[]{:S(2)}) async-start(), calls=%async_computation.4 | async-start | bytes 10485760 | tf_op jit(solution)/shard_map/all_gather | solution.py:100
  7.3 183.2 %reduce-scatter.2.cloned.1.call-start = ((), (), s32[]{:S(2)}) async-start(), calls=%async_computation.5 | async-start | bytes 1310720 | tf_op jit(solution)/shard_map/reduce_scatter | solution.py:105
  9.6 157.7 %copy-start.6 = (s32[64,8]{0,1:T(8,128)S(1)}, s32[64,8]{0,1:T(8,128)}, u32[]{:S(2)}) copy-start(s32[64,8]{0,1:T(8,128)} %param.23) | copy-start | bytes 6148
  9.6 180.8 %copy-start.4 = (bf16[64,4096]{1,0:T(8,128)(2,1)S(1)}, bf16[64,4096]{1,0:T(8,128)(2,1)}, u32[]{:S(2)}) copy-start(bf16[64,4096]{1,0:T(8,128)(2,1)} %param.13) | copy-start | bytes 1572868
  9.7 181.9 %copy-start.5 = (f32[4096]{0:T(1024)S(1)}, f32[4096]{0:T(1024)}, u32[]{:S(2)}) copy-start(f32[4096]{0:T(1024)} %param.19) | copy-start | bytes 49156
  167.3 218.3 %all-gather.5.cloned.1.call-start = ((), (), s32[]{:S(2)}) async-start(), calls=%async_computation.6 | async-start | bytes 2621440 | tf_op jit(solution)/shard_map/all_gather | solution.py:129
  247.1 25.5 %collective-permute-start = (bf16[4,8,1,8,4096]{4,3,1,0,2:T(8,128)(2,1)S(1)}, bf16[4,8,1,8,4096]{4,3,1,0,2:T(8,128)(2,1)S(1)}, u32[]{:S(2)}, u32[]{:S(2)}) collective-permute-start(bf16[4,8,1,8,4096]{4,3,1,0,2:T(8,128)(2,1)S(1)} %bitcast.132), channel_id=1, source_target_pairs={{0,1},{1,2},{2,3},{3,0},{4,5},{5,6},{6,7},{7,4},{8,9},{9,10},{10,1... | collective-permute-start | bytes 6291464 | tf_op jit(solution)/shard_map/ppermute | solution.py:22
  272.6 25.5 %collective-permute-start.1 = (bf16[4,8,1,8,4096]{4,3,1,0,2:T(8,128)(2,1)S(1)}, bf16[4,8,1,8,4096]{4,3,1,0,2:T(8,128)(2,1)S(1)}, u32[]{:S(2)}, u32[]{:S(2)}) collective-permute-start(bf16[4,8,1,8,4096]{4,3,1,0,2:T(8,128)(2,1)S(1)} %collective-permute-done), channel_id=1, source_target_pairs={{0,1},{1,2},{2,3},{3,0},{4,5},{5,6},{6,7},{7,4},{8,9},{9,10},{10,1... | collective-permute-start | bytes 6291464 | tf_op jit(solution)/shard_map/ppermute | solution.py:22
  298.1 25.5 %collective-permute-start.2 = (bf16[4,8,1,8,4096]{4,3,1,0,2:T(8,128)(2,1)S(1)}, bf16[4,8,1,8,4096]{4,3,1,0,2:T(8,128)(2,1)S(1)}, u32[]{:S(2)}, u32[]{:S(2)}) collective-permute-start(bf16[4,8,1,8,4096]{4,3,1,0,2:T(8,128)(2,1)S(1)} %collective-permute-done.1), channel_id=1, source_target_pairs={{0,1},{1,2},{2,3},{3,0},{4,5},{5,6},{6,7},{7,4},{8,9},{9,10},{10,1... | collective-permute-start | bytes 6291464 | tf_op jit(solution)/shard_map/ppermute | solution.py:22
  447.6 5.2 %copy-start.7 = (f32[64,8]{0,1:T(8,128)S(1)}, f32[64,8]{0,1:T(8,128)}, u32[]{:S(2)}) copy-start(f32[64,8]{0,1:T(8,128)} %param.24) | copy-start | bytes 6148
  449.2 29.2 %all-to-all-start.2 = ((bf16[4,8,4,8,1024]{4,3,0,1,2:T(8,128)(2,1)}), bf16[4,8,4,8,1024]{4,3,0,1,2:T(8,128)(2,1)S(1)}, u32[]{:S(2)}, u32[]{:S(2)}) async-start(bf16[4,8,4,8,1024]{4,3,0,1,2:T(8,128)(2,1)} %copy.43), calls=%async_computation.3 | async-start | bytes 4194304 | tf_op jit(solution)/shard_map/all_to_all | solution.py:134
  478.4 1.4 copy-start.2
  481.6 3.7 copy-start.1
  481.6 2.0 copy-start.3
Sparse Core Ops, SparseCore 0:
  8.9 152.3 all-gather.2
  167.4 22.9 reduce-scatter.1
  364.7 20.9 all-gather.4
